TPU v7x, 256 devices: a whole 4x4x8 slice. The times are simulated.
256 devices in a mesh: tm: 8 (over y_hi, x), stream: 32 (over y_lo, z, core).
Axes of the slice: x: 4, y: 4 (y_hi: 2, y_lo: 2; y = y_hi * 2 + y_lo), z: 8, core: 2. Of those that a mesh axis runs over, the one named last changes fastest.
Arguments:
- tokens: bfloat16 [32, 1024, 768], P('stream', 'tm'), may hold values from -6 to 6
- cotangent: bfloat16 [32, 1024, 768], P('stream', 'tm'), may hold values from -6 to 6
- decay: float32 [32, 1024, 24], P('stream', 'tm'), may hold values from 0.4 to 1, as said below
- in_w: bfloat16 [768, 3328], P('stream'), may hold values from -0.21875 to 0.21875
- out_w: bfloat16 [1536, 768], P('stream'), may hold values from -0.15625 to 0.15625
- conv_w: float32 [4, 1792], replicated, may hold values from -3 to 3
- dskip: float32 [24], replicated, may hold values from 0.5 to 2
- norm_w: float32 [1536], replicated, may hold values from 0.1 to 1.9
Outputs:
- out: bfloat16 [32, 1024, 768], P('stream', 'tm')
- grad_tokens: bfloat16 [32, 1024, 768], P('stream', 'tm')
- grad_out_t: float32 [768, 1536], P(('tm', 'stream'))
Inputs may be any that keep to these rules, and one draw needn't show every extreme that they name: decay lies strictly between 0 and 1.
All inputs are finite; a program needn't handle non-finite values.
Results may differ from a plain program's by a relative error of at most 0.015.
Values may be sent and summed in bfloat16 or wider, within the bound.
No kernel may reach another device: no remote copies, remote signals or barrier semaphores. Data moves between devices by JAX's collectives and lax.ppermute only.
A program may use at most 128 MiB of HBM per device.

v0:
```python
import jax
import jax.numpy as jnp
from jax import lax
from jax.sharding import PartitionSpec as P

block_len = 128
working = lax.Precision.HIGH


def shifted(value, axis, steps):
    count = lax.axis_size(axis)
    initial, last = (max(0, -steps), min(count, count - steps))
    return lax.ppermute(value, axis, [(source, source + steps) for source in range(initial, last)])


def entering(value, axis, join, neutral):
    count, mine = (lax.axis_size(axis), lax.axis_index(axis))
    pieces = jax.tree.map(lambda part: lax.all_gather(part, axis), value)
    running = jax.tree.map(
        lambda part, zero: jnp.full_like(part, 0) + jnp.asarray(zero, part.dtype), value, neutral
    )

    def step(position, running):
        longer = join(running, jax.tree.map(lambda part: part[position], pieces))
        return jax.tree.map(lambda new, old: jnp.where(position < mine, new, old), longer, running)

    return lax.fori_loop(0, count - 1, step, running)


def carried_in(shard, axis, join, neutral):
    count = lax.axis_size(axis)
    place = lax.axis_index(axis)
    ahead = count - 1 - place
    gathered = jax.tree.map(
        lambda a, kind: lax.all_gather(a.astype(kind), axis),
        shard,
        jax.tree.map(lambda a: jnp.bfloat16 if a.dtype == jnp.float32 else a.dtype, shard),
    )
    state = jax.tree.map(lambda a, e: jnp.zeros_like(a) + jnp.asarray(e, a.dtype), shard, neutral)

    def one(step, state):
        source = count - 1 - step
        return join(
            state,
            jax.tree.map(
                lambda a, own: lax.dynamic_index_in_dim(a, source, 0, False).astype(own.dtype),
                gathered,
                shard,
            ),
        )

    return lax.fori_loop(0, ahead, one, state)


def conv_apply(extended, conv_weight):
    conv_taps = conv_weight.shape[0]
    row_count = extended.shape[0] - conv_taps + 1
    result = jnp.zeros((row_count, extended.shape[1]), jnp.float32)
    for offset in range(conv_taps):
        result = result + conv_weight[offset] * extended[offset : offset + row_count]
    return result


def block_ssm(carry_state, x_block, b_block, c_block, decay_log):
    cumulative = jnp.cumsum(decay_log, axis=0)
    carried = jnp.exp(cumulative)[:, :, None] * jnp.einsum(
        "tn,hpn->thp", c_block, carry_state, precision=working
    )
    scores = jnp.einsum("tn,sn->ts", c_block, b_block, precision=working)
    later_idx = lax.broadcasted_iota(jnp.int32, scores.shape, 0)
    earlier_idx = lax.broadcasted_iota(jnp.int32, scores.shape, 1)
    causal = (later_idx >= earlier_idx)[:, :, None]
    log_gap = cumulative[:, None, :] - cumulative[None, :, :]
    weight = jnp.where(causal, jnp.exp(jnp.where(causal, log_gap, 0.0)), 0.0) * scores[:, :, None]
    inside = jnp.einsum("tsh,shp->thp", weight, x_block, precision=working)
    fade_out = jnp.exp(cumulative[-1][None, :] - cumulative)
    added = jnp.einsum("shp,sn->hpn", fade_out[:, :, None] * x_block, b_block, precision=working)
    carry_state = jnp.exp(cumulative[-1])[:, None, None] * carry_state + added
    return (carried + inside, carry_state)


def local_scan(conv_out, decay_log, skip_gain, head_count, state_width):
    row_count = conv_out.shape[0]
    inner_width = conv_out.shape[1] - 2 * state_width
    head_dim = inner_width // head_count
    block_rows = min(block_len, row_count)
    blocks = row_count // block_rows
    x_all = conv_out[:, :inner_width].reshape(blocks, block_rows, head_count, head_dim)
    b_all = conv_out[:, inner_width : inner_width + state_width].reshape(
        blocks, block_rows, state_width
    )
    c_all = conv_out[:, inner_width + state_width :].reshape(blocks, block_rows, state_width)
    d_all = decay_log.reshape(blocks, block_rows, head_count)

    def advance(carry_state, pieces):
        outputs, carry_state = block_ssm(carry_state, pieces[0], pieces[1], pieces[2], pieces[3])
        return (carry_state, outputs)

    start_state = jnp.zeros((head_count, head_dim, state_width), jnp.float32)
    final_state, results = lax.scan(advance, start_state, (x_all, b_all, c_all, d_all))
    x_heads = conv_out[:, :inner_width].reshape(row_count, head_count, head_dim)
    outputs = results.reshape(row_count, head_count, head_dim) + skip_gain[None, :, None] * x_heads
    return (outputs.reshape(row_count, inner_width), final_state)


def gate_norm(ssm_out, gate_in, norm_gain):
    gated = ssm_out * jax.nn.silu(gate_in)
    factor = lax.rsqrt(jnp.mean(gated * gated, axis=-1, keepdims=True) + 1e-05)
    return gated * factor * norm_gain


def combine_carry(earlier, later):
    return (earlier[0] * later[0], later[0][:, None, None] * earlier[1] + later[1])


def shards(tokens, cotangent, decay, in_w, out_w, conv_w, dskip, norm_w):
    inputs = tokens[0]
    grad_out = cotangent[0]
    decay_log = jnp.log(decay[0])
    row_count = inputs.shape[0]
    head_count = dskip.shape[0]
    full_in, full_out = (
        lax.all_gather(in_w, "stream", axis=0, tiled=True),
        lax.all_gather(out_w, "stream", axis=0, tiled=True),
    )
    inner_width = full_out.shape[0]
    proj_width = full_in.shape[1]
    state_width = (proj_width - 2 * inner_width) // 2
    head_dim = inner_width // head_count
    conv_taps = conv_w.shape[0]
    projected = jnp.dot(inputs, full_in, preferred_element_type=jnp.float32).astype(jnp.bfloat16)
    gate_in = projected[:, :inner_width].astype(jnp.float32)
    mix_in = projected[:, inner_width:]
    rim_rows = shifted(mix_in[row_count - conv_taps + 1 :], "tm", 1)
    extended = jnp.concatenate([rim_rows, mix_in], axis=0).astype(jnp.float32)

    def conv_part(values):
        return conv_apply(values, conv_w)

    pre_act, conv_back = jax.vjp(conv_part, extended)
    conv_low = jax.nn.silu(pre_act).astype(jnp.bfloat16)
    conv_out = lax.optimization_barrier(conv_low).astype(jnp.float32)

    def scan_part(values):
        return local_scan(values, decay_log, dskip, head_count, state_width)

    (ssm_local, state_local), ssm_back = jax.vjp(scan_part, conv_out)
    cumulative = jnp.cumsum(decay_log, axis=0)
    decay_total = jnp.exp(cumulative[-1])
    identity = (jnp.ones_like(decay_total), jnp.zeros_like(state_local))
    state_in = entering((decay_total, state_local), "tm", combine_carry, identity)[1]
    b_vecs = conv_out[:, inner_width : inner_width + state_width]
    c_vecs = conv_out[:, inner_width + state_width :]
    x_heads = conv_out[:, :inner_width].reshape(row_count, head_count, head_dim)
    growth = jnp.exp(cumulative)
    carried = growth[:, :, None] * jnp.einsum("tn,hpn->thp", c_vecs, state_in, precision=working)
    ssm_out = ssm_local + carried.reshape(row_count, inner_width)

    def norm_part(ssm_values, gate_values):
        return gate_norm(ssm_values, gate_values, norm_w)

    normed, norm_back = jax.vjp(norm_part, ssm_out, gate_in)
    normed_low = normed.astype(jnp.bfloat16)
    result = jnp.dot(normed_low, full_out, preferred_element_type=jnp.float32).astype(jnp.bfloat16)
    grad_normed = jnp.einsum("td,ed->te", grad_out, full_out, preferred_element_type=jnp.float32)
    grad_ssm, grad_gate = norm_back(grad_normed)
    grad_heads = grad_ssm.reshape(row_count, head_count, head_dim)
    weighted = growth[:, :, None] * grad_heads
    adjoint_local = jnp.einsum("thp,tn->hpn", weighted, c_vecs, precision=working)
    adjoint_in = carried_in((decay_total, adjoint_local), "tm", combine_carry, identity)[1]
    (grad_local,) = ssm_back((grad_ssm, jnp.zeros_like(state_local)))
    fade_out = jnp.exp(cumulative[-1][None, :] - cumulative)
    grad_x = fade_out[:, :, None] * jnp.einsum("hpn,tn->thp", adjoint_in, b_vecs, precision=working)
    grad_b = jnp.einsum(
        "thp,hpn->tn", fade_out[:, :, None] * x_heads, adjoint_in, precision=working
    )
    grad_c = jnp.einsum("thp,hpn->tn", weighted, state_in, precision=working)
    grad_conv = grad_local + jnp.concatenate(
        [grad_x.reshape(row_count, inner_width), grad_b, grad_c], axis=1
    )
    sigmoid_pre = jax.nn.sigmoid(pre_act)
    (grad_ext,) = conv_back(grad_conv * sigmoid_pre * (1.0 + pre_act * (1.0 - sigmoid_pre)))
    incoming = shifted(grad_ext[: conv_taps - 1], "tm", -1)
    grad_mix = grad_ext[conv_taps - 1 :] + jnp.pad(
        incoming, ((row_count - conv_taps + 1, 0), (0, 0))
    )
    grad_proj = jnp.concatenate([grad_gate, grad_mix], axis=1).astype(jnp.bfloat16)
    grad_tokens = jnp.einsum(
        "tj,dj->td", grad_proj, full_in, preferred_element_type=jnp.float32
    ).astype(jnp.bfloat16)
    n_time = lax.axis_size("tm")
    n_stream = lax.axis_size("stream")
    grad_scale = (n_time * n_stream * row_count) ** (-0.5)
    summed = lax.psum_scatter(
        jnp.einsum("td,te->de", grad_out, normed_low, preferred_element_type=jnp.float32),
        ("tm", "stream"),
        scatter_dimension=0,
        tiled=True,
    )
    return (result[None], grad_tokens[None], summed * grad_scale)


def solution(mesh):
    in_specs = (
        P("stream", "tm", None),
        P("stream", "tm", None),
        P("stream", "tm", None),
        P("stream", None),
        P("stream", None),
        P(),
        P(),
        P(),
    )
    out_specs = (P("stream", "tm", None), P("stream", "tm", None), P(("tm", "stream"), None))
    return jax.shard_map(shards, mesh=mesh, in_specs=in_specs, out_specs=out_specs, check_vma=False)
```

profile of v0, /device:TPU:32, one launch (start us, length us, event | category | flops | bytes accessed | tf_op | source)
XLA Modules:
  0.0 630.5 jit_solution(17365361491446200378)
XLA Ops:
  9.0 70.2 %all-gather.9.cloned.1.call-done = bf16[768,3328]{1,0:T(8,128)(2,1)} async-done(((bf16[24,3328]{1,0:T(8,128)(2,1)}), bf16[768,3328]{1,0:T(8,128)(2,1)}) %all-gather.9.cloned.1.call-update) | async-done | bytes 5111824 | tf_op jit(solution)/shard_map/all_gather | solution.py:123
  79.2 3.4 convolution_convert_fusion
  82.7 3.4 collective-permute-start
  87.5 1.5 multiply_convert_fusion
  89.5 1.3 convolution_add_fusion
  91.8 24.1 %all-gather.2 = f32[8,1,24]{2,1,0:T(1,128)S(1)} all-gather(f32[1,1,24]{2,1,0:T(1,128)S(1)} %get-tuple-element.413), channel_id=1, replica_groups=mesh['tm'=8,'stream'=32] {'tm'}, dimensions={0}, use_global_device_ids=true | all-gather | bytes 864 | tf_op jit(solution)/shard_map/all_gather | solution.py:18
  117.0 2.3 fusion.7
  120.8 67.1 %all-gather.13.cloned.1.call-done = f32[192,64,128]{2,1,0:T(8,128)} async-done(((f32[24,64,128]{2,1,0:T(8,128)}), f32[192,64,128]{2,1,0:T(8,128)}) %all-gather.13.cloned.1.call-update) | async-done | bytes 6291472 | tf_op jit(solution)/shard_map/all_gather | solution.py:18
  187.9 9.4 %while.21 = (s32[]{:T(128)}, f32[24,64,128]{2,1,0:T(8,128)S(1)}, s32[]{:T(128)}, f32[8,24]{1,0:T(8,128)S(1)}, f32[8,24,64,128]{3,2,1,0:T(8,128)}, /*index=5*/s32[]{:T(128)}, s32[]{:T(128)}) while((s32[]{:T(128)}, f32[24,64,128]{2,1,0:T(8,128)S(1)}, s32[]{:T(128)}, f32[8,24]{1,0:T(8,128)S(1)}, f32[8,24,64,128]{3,2,1,0:T(8,128)}, ...), condition=%wide.region_2.3_spmd.clone, body=%wide.region_1.2_spmd.clone.sunk | while | flops 786436 | bytes 2359697 | solution.py:27
  187.9 1.3 fusion.109
  189.2 1.3 fusion.109
  190.6 1.3 fusion.109
  191.9 1.3 fusion.109
  193.3 1.3 fusion.109
  194.6 1.3 fusion.109
  196.0 1.3 fusion.109
  198.8 52.8 %all-gather.11.cloned.1.call-done = bf16[1536,768]{1,0:T(8,128)(2,1)} async-done(((bf16[48,768]{1,0:T(8,128)(2,1)}), bf16[1536,768]{1,0:T(8,128)(2,1)}) %all-gather.11.cloned.1.call-update) | async-done | bytes 2359312 | tf_op jit(solution)/shard_map/all_gather | solution.py:124
  251.7 4.0 multiply_reduce_fusion
  255.7 3.0 convolution_bitcast_fusion
  258.8 3.5 broadcast_multiply_fusion.4
  262.6 1.9 convolution_convert_fusion.1
  264.5 23.2 %all-gather.3 = bf16[8,1,24]{2,1,0:T(2,128)(2,1)S(1)} all-gather(bf16[1,1,24]{2,1,0:T(2,128)(2,1)S(1)} %get-tuple-element.411), channel_id=1, replica_groups=mesh['tm'=8,'stream'=32] {'tm'}, dimensions={0}, use_global_device_ids=true | all-gather | bytes 432 | tf_op jit(solution)/shard_map/all_gather | solution.py:35
  288.7 2.3 copy.57
  292.9 2.1 fusion.14
  294.9 2.3 copy.59
  297.2 2.1 mul.434
  299.4 1.4 copy.58
  302.4 1.3 fusion.1
  303.7 1.6 convolution_add_fusion.1
  305.3 1.5 convolution_add_fusion.2
  306.9 1.2 fusion.15
  308.1 221.1 %all-reduce.12.cloned.1.call-done = f32[768,1536]{0,1:T(8,128)} async-done(((f32[768,1536]{0,1:T(8,128)}), f32[768,1536]{0,1:T(8,128)}) %all-reduce.12.cloned.1.call-update) | async-done | bytes 4718608
  529.2 1.7 dynamic-slice_multiply_fusion
  531.8 68.9 %all-gather.15.cloned.1.call-done = bf16[192,64,128]{2,1,0:T(8,128)(2,1)} async-done(((bf16[24,64,128]{2,1,0:T(8,128)(2,1)}), bf16[192,64,128]{2,1,0:T(8,128)(2,1)}) %all-gather.15.cloned.1.call-update) | async-done | bytes 3145744 | tf_op jit(solution)/shard_map/all_gather | solution.py:35
  600.8 8.7 %while.20 = (s32[]{:T(128)}, f32[24,64,128]{2,1,0:T(8,128)S(1)}, s32[]{:T(128)}, bf16[8,24]{1,0:T(8,128)(2,1)S(1)}, bf16[8,24,64,128]{3,2,1,0:T(8,128)(2,1)}, /*index=5*/s32[]{:T(128)}, s32[]{:T(128)}, s32[]{:T(128)}, s32[]{:T(128)}) while((s32[]{:T(128)}, f32[24,64,128]{2,1,0:T(8,128)S(1)}, s32[]{:T(128)}, bf16[8,24]{1,0:T(8,128)(2,1)S(1)}, ...), condition=%wide.region_7.8_spmd, body=%wide.region_6.7_spmd.sunk | while | flops 589854 | bytes 1966475 | solution.py:52
  600.8 1.2 convert_add_fusion.2
  602.1 1.2 convert_add_fusion.2
  603.3 1.2 convert_add_fusion.2
  604.6 1.2 convert_add_fusion.2
  605.8 1.2 convert_add_fusion.2
  607.1 1.2 convert_add_fusion.2
  608.3 1.2 convert_add_fusion.2
  609.5 1.4 convolution_bitcast_fusion.2
  611.0 1.3 convolution_multiply_fusion.1
  613.5 1.6 broadcast_multiply_fusion
  615.4 1.6 collective-permute-start.1
  617.2 4.2 collective-permute-done.1
  621.5 2.5 fusion.16
  (112 shorter events, 16.5 us)
Async XLA Ops:
  7.2 244.5 %copy-start = (bf16[1,128,768]{2,1,0:T(8,128)(2,1)S(1)}, bf16[1,128,768]{2,1,0:T(8,128)(2,1)}, u32[]{:S(2)}) copy-start(bf16[1,128,768]{2,1,0:T(8,128)(2,1)} %param.13) | copy-start | bytes 589828
  7.2 72.0 %all-gather.9.cloned.1.call-start = ((), (), s32[]{:S(2)}) async-start(), calls=%async_computation | async-start | bytes 5271552 | tf_op jit(solution)/shard_map/all_gather | solution.py:123
  7.9 180.0 %all-gather.13.cloned.1.call-start = ((), (), s32[]{:S(2)}) async-start(), calls=%async_computation.2 | async-start | bytes 7077888 | tf_op jit(solution)/shard_map/all_gather | solution.py:18
  9.0 77.0 %copy-start.19 = (f32[4,1792]{1,0:T(4,128)S(1)}, f32[4,1792]{1,0:T(4,128)}, u32[]{:S(2)}) copy-start(f32[4,1792]{1,0:T(4,128)} %param.17) | copy-start | bytes 86020
  82.6 6.6 %copy-start.5 = (bf16[128,3328]{1,0:T(8,128)(2,1)}, bf16[128,3328]{1,0:T(8,128)(2,1)S(1)}, u32[]{:S(2)}) copy-start(bf16[128,3328]{1,0:T(8,128)(2,1)S(1)} %convolution_convert_fusion) | copy-start | bytes 2555908
  82.7 4.8 collective-permute-start
  86.1 2.9 copy-start.11
  86.1 2.9 copy-start.13
  86.1 2.9 copy-start.15
  86.2 2.9 copy-start.17
  89.1 162.6 %copy-start.3 = (bf16[128,1792]{1,0:T(8,128)(2,1)}, bf16[128,1792]{1,0:T(8,128)(2,1)S(1)}, u32[]{:S(2)}) copy-start(bf16[128,1792]{1,0:T(8,128)(2,1)S(1)} %get-tuple-element.403) | copy-start | bytes 1376260
  89.5 2.2 copy-start.20
  90.8 160.9 %all-gather.11.cloned.1.call-start = ((), (), s32[]{:S(2)}) async-start(), calls=%async_computation.1 | async-start | bytes 2433024 | tf_op jit(solution)/shard_map/all_gather | solution.py:124
  91.5 437.7 %all-reduce.12.cloned.1.call-start = ((), (), s32[]{:S(2)}) async-start(), calls=%async_computation.4 | async-start | bytes 9437184
  197.3 54.4 %copy-start.18 = (f32[1536]{0:T(1024)S(1)}, f32[1536]{0:T(1024)}, u32[]{:S(2)}) copy-start(f32[1536]{0:T(1024)} %param.19) | copy-start | bytes 18436
  255.7 3.1 copy-start.1
  258.8 342.0 %all-gather.15.cloned.1.call-start = ((), (), s32[]{:S(2)}) async-start(), calls=%async_computation.3 | async-start | bytes 3538944 | tf_op jit(solution)/shard_map/all_gather | solution.py:35
  300.8 1.6 copy-start.10
  302.4 4.5 copy-start.2
  302.4 4.5 copy-start.8
  611.0 2.4 copy-start.4
  611.0 2.4 copy-start.6
  612.2 1.2 copy-start.7
  613.4 1.7 copy-start.12
  613.4 1.7 copy-start.14
  613.4 1.7 copy-start.16
  615.1 6.4 %slice-start = ((s8[5111808]{0:T(1024)(128)(4,1)}), s8[4194304]{0:T(1024)(128)(4,1)S(1)}, s32[]{:S(2)}) async-start(s8[5111808]{0:T(1024)(128)(4,1)} %bitcast.117), calls=%async_computation.5 | async-start | bytes 8388608
  615.3 6.2 slice-start.1
  615.4 6.2 copy-start.9
  615.4 6.0 collective-permute-start.1
Sparse Core Ops, SparseCore 0:
  9.8 69.3 all-gather.8
  90.9 96.9 all-gather.12
  189.8 61.8 all-gather.10
  258.9 270.3 all-reduce.11
  531.7 68.9 all-gather.14
where the time goes:
time: 632 us; the launch traced here: 631 us
  waiting for transfers between devices  487 us (77%)
  blocking collectives  47.3 us (7%)
  matrix products  33.2 us (5%)
  other arithmetic  29.1 us (5%)
  between operations  14.3 us (2%)
  local copies, waits for them, and re-layouts  14.2 us (2%)
    unnamed x6, waiting for transfers between devices  223 us
    all_gather x1, waiting for transfers between devices, shards(): lax.all_gather(in_w, 'stream', axis=0, tiled=True)  70.2 us
    all_gather x1, waiting for transfers between devices, carried_in(): lax.all_gather(a.astype(kind), axis)  68.9 us
    all_gather x1, waiting for transfers between devices, entering(): pieces = jax.tree.map(lambda part: lax.all_gather(part, axis), value)  67.1 us
    all_gather x1, waiting for transfers between devices, shards(): lax.all_gather(out_w, 'stream', axis=0, tiled=True)  52.8 us
    all_gather x1, blocking collectives, entering(): pieces = jax.tree.map(lambda part: lax.all_gather(part, axis), value)  24.1 us
    all_gather x1, blocking collectives, carried_in(): lax.all_gather(a.astype(kind), axis)  23.2 us
  transfers between devices with their start and end apart: 7, of which 7 were waited for; matrix products, arithmetic and copies ran while one was open for 7% of the time, Pallas kernels for 0%

commit v1 on v0

--- a/solution.py
+++ b/solution.py
@@ -5,6 +5,11 @@
 
 block_len = 128
 working = lax.Precision.HIGH
+
+
+def exchange_gather(x, axis, dim):
+    sent = jnp.stack([x] * lax.axis_size(axis))
+    return jnp.concatenate(lax.all_to_all(sent, axis, 0, 0), axis=dim)
 
 
 def shifted(value, axis, steps):
@@ -121,7 +126,7 @@
     head_count = dskip.shape[0]
     full_in, full_out = (
         lax.all_gather(in_w, "stream", axis=0, tiled=True),
-        lax.all_gather(out_w, "stream", axis=0, tiled=True),
+        exchange_gather(out_w, "stream", 0),
     )
     inner_width = full_out.shape[0]
     proj_width = full_in.shape[1]

time: 632 us -> 592 us (0.937)
  waiting for transfers between devices: 487 us -> 436 us
  starting transfers between devices: 5.12 us -> 12.7 us
    all_gather x1 -> x0, waiting for transfers between devices: 52.8 us -> none  [shards(): lax.all_gather(out_w, 'stream', axis=0, tiled=True)]
    all_to_all x0 -> x1, starting transfers between devices: none -> 7.66 us  [exchange_gather(): return jnp.concatenate(lax.all_to_all(sent, axis, 0, 0), axis=dim)]
    unnamed x6 -> x5, waiting for transfers between devices: 223 us -> 221 us
  transfers between devices with their start and end apart: 7 -> 7, of which waited for: 7 -> 6; matrix products, arithmetic and copies ran while one was open for 7% -> 8% of each run, Pallas kernels for 0% -> 0%
where the time goes in v1:
time: 592 us; the launch traced here: 590 us
  waiting for transfers between devices  436 us (74%)
  blocking collectives  45.1 us (8%)
  matrix products  34.9 us (6%)
  other arithmetic  30 us (5%)
  local copies, waits for them, and re-layouts  17.1 us (3%)
  between operations  14.3 us (2%)
  starting transfers between devices  12.7 us (2%)
    unnamed x5, waiting for transfers between devices  221 us
    all_gather x1, waiting for transfers between devices, shards(): lax.all_gather(in_w, 'stream', axis=0, tiled=True)  70.2 us
    all_gather x1, waiting for transfers between devices, entering(): pieces = jax.tree.map(lambda part: lax.all_gather(part, axis), value)  70.1 us
    all_gather x1, waiting for transfers between devices, carried_in(): lax.all_gather(a.astype(kind), axis)  68.9 us
    all_gather x1, blocking collectives, entering(): pieces = jax.tree.map(lambda part: lax.all_gather(part, axis), value)  24 us
    all_gather x1, blocking collectives, carried_in(): lax.all_gather(a.astype(kind), axis)  21.1 us
  transfers between devices with their start and end apart: 7, of which 6 were waited for; matrix products, arithmetic and copies ran while one was open for 8% of the time, Pallas kernels for 0%

profile of v1, /device:TPU:32, one launch (start us, length us, event | category | flops | bytes accessed | tf_op | source)
XLA Modules:
  0.0 590.3 jit_solution(8418887914674219678)
XLA Ops:
  9.0 70.2 %all-gather.8.cloned.1.call-done = bf16[768,3328]{1,0:T(8,128)(2,1)} async-done(((bf16[24,3328]{1,0:T(8,128)(2,1)}), bf16[768,3328]{1,0:T(8,128)(2,1)}) %all-gather.8.cloned.1.call-update) | async-done | bytes 5111824 | tf_op jit(solution)/shard_map/all_gather | solution.py:128
  79.2 3.4 convolution_convert_fusion
  82.7 3.4 collective-permute-start
  87.5 1.5 multiply_convert_fusion
  90.1 1.4 copy.54
  91.5 1.3 convolution_add_fusion
  92.8 1.7 stack.2
  94.5 7.7 %all-to-all-start = ((bf16[32,48,768]{2,1,0:T(8,128)(2,1)}), bf16[32,48,768]{2,1,0:T(8,128)(2,1)}, u32[]{:S(2)}, u32[]{:S(2)}) async-start(bf16[32,48,768]{2,1,0:T(8,128)(2,1)} %stack.2), calls=%async_computation | async-start | bytes 4718592 | tf_op jit(solution)/shard_map/all_to_all | solution.py:12
  102.5 24.0 %all-gather.2 = f32[8,1,24]{2,1,0:T(1,128)S(1)} all-gather(f32[1,1,24]{2,1,0:T(1,128)S(1)} %get-tuple-element.413), channel_id=1, replica_groups=mesh['tm'=8,'stream'=32] {'tm'}, dimensions={0}, use_global_device_ids=true | all-gather | bytes 864 | tf_op jit(solution)/shard_map/all_gather | solution.py:23
  127.5 2.3 fusion.7
  131.4 70.1 %all-gather.10.cloned.1.call-done = f32[192,64,128]{2,1,0:T(8,128)} async-done(((f32[24,64,128]{2,1,0:T(8,128)}), f32[192,64,128]{2,1,0:T(8,128)}) %all-gather.10.cloned.1.call-update) | async-done | bytes 6291472 | tf_op jit(solution)/shard_map/all_gather | solution.py:23
  201.5 9.4 %while.21 = (s32[]{:T(128)}, f32[24,64,128]{2,1,0:T(8,128)S(1)}, s32[]{:T(128)}, f32[8,24]{1,0:T(8,128)S(1)}, f32[8,24,64,128]{3,2,1,0:T(8,128)}, /*index=5*/s32[]{:T(128)}, s32[]{:T(128)}) while((s32[]{:T(128)}, f32[24,64,128]{2,1,0:T(8,128)S(1)}, s32[]{:T(128)}, f32[8,24]{1,0:T(8,128)S(1)}, f32[8,24,64,128]{3,2,1,0:T(8,128)}, ...), condition=%wide.region_2.3_spmd.clone, body=%wide.region_1.2_spmd.clone.sunk | while | flops 786436 | bytes 2359697 | solution.py:32
  201.5 1.3 fusion.109
  202.8 1.3 fusion.109
  204.2 1.3 fusion.109
  205.5 1.3 fusion.109
  206.9 1.3 fusion.109
  208.2 1.3 fusion.109
  209.6 1.3 fusion.109
  212.5 4.0 multiply_reduce_fusion
  216.5 3.0 convolution_bitcast_fusion
  219.6 3.5 broadcast_multiply_fusion.4
  223.4 1.9 convolution_convert_fusion.1
  225.3 21.1 %all-gather.3 = bf16[8,1,24]{2,1,0:T(2,128)(2,1)S(1)} all-gather(bf16[1,1,24]{2,1,0:T(2,128)(2,1)S(1)} %get-tuple-element.411), channel_id=1, replica_groups=mesh['tm'=8,'stream'=32] {'tm'}, dimensions={0}, use_global_device_ids=true | all-gather | bytes 432 | tf_op jit(solution)/shard_map/all_gather | solution.py:40
  247.4 2.3 copy.57
  251.6 2.1 fusion.14
  253.6 2.3 copy.59
  256.0 2.1 mul.434
  258.1 1.4 copy.58
  261.1 1.3 fusion.1
  262.5 1.6 convolution_add_fusion.1
  264.1 1.5 convolution_add_fusion.2
  265.6 2.9 fusion.15
  268.5 220.5 %all-reduce.12.cloned.1.call-done = f32[768,1536]{0,1:T(8,128)} async-done(((f32[768,1536]{0,1:T(8,128)}), f32[768,1536]{0,1:T(8,128)}) %all-reduce.12.cloned.1.call-update) | async-done | bytes 4718608
  489.0 1.7 dynamic-slice_multiply_fusion
  491.6 68.9 %all-gather.12.cloned.1.call-done = bf16[192,64,128]{2,1,0:T(8,128)(2,1)} async-done(((bf16[24,64,128]{2,1,0:T(8,128)(2,1)}), bf16[192,64,128]{2,1,0:T(8,128)(2,1)}) %all-gather.12.cloned.1.call-update) | async-done | bytes 3145744 | tf_op jit(solution)/shard_map/all_gather | solution.py:40
  560.6 8.7 %while.20 = (s32[]{:T(128)}, f32[24,64,128]{2,1,0:T(8,128)S(1)}, s32[]{:T(128)}, bf16[8,24]{1,0:T(8,128)(2,1)S(1)}, bf16[8,24,64,128]{3,2,1,0:T(8,128)(2,1)}, /*index=5*/s32[]{:T(128)}, s32[]{:T(128)}, s32[]{:T(128)}, s32[]{:T(128)}) while((s32[]{:T(128)}, f32[24,64,128]{2,1,0:T(8,128)S(1)}, s32[]{:T(128)}, bf16[8,24]{1,0:T(8,128)(2,1)S(1)}, ...), condition=%wide.region_7.8_spmd, body=%wide.region_6.7_spmd.sunk | while | flops 589854 | bytes 1966475 | solution.py:57
  560.6 1.2 convert_add_fusion.2
  561.9 1.2 convert_add_fusion.2
  563.1 1.2 convert_add_fusion.2
  564.3 1.2 convert_add_fusion.2
  565.6 1.2 convert_add_fusion.2
  569.3 1.4 convolution_bitcast_fusion.2
  570.7 1.3 convolution_multiply_fusion.1
  573.2 1.6 broadcast_multiply_fusion
  575.2 1.6 collective-permute-start.1
  577.0 4.2 collective-permute-done.1
  581.3 2.5 fusion.16
  (112 shorter events, 18.9 us)
Async XLA Ops:
  7.2 205.3 %copy-start = (bf16[1,128,768]{2,1,0:T(8,128)(2,1)S(1)}, bf16[1,128,768]{2,1,0:T(8,128)(2,1)}, u32[]{:S(2)}) copy-start(bf16[1,128,768]{2,1,0:T(8,128)(2,1)} %param.13) | copy-start | bytes 589828
  7.2 72.0 %all-gather.8.cloned.1.call-start = ((), (), s32[]{:S(2)}) async-start(), calls=%async_computation.1 | async-start | bytes 5271552 | tf_op jit(solution)/shard_map/all_gather | solution.py:128
  7.9 193.6 %all-gather.10.cloned.1.call-start = ((), (), s32[]{:S(2)}) async-start(), calls=%async_computation.2 | async-start | bytes 7077888 | tf_op jit(solution)/shard_map/all_gather | solution.py:23
  9.0 77.0 %copy-start.19 = (f32[4,1792]{1,0:T(4,128)S(1)}, f32[4,1792]{1,0:T(4,128)}, u32[]{:S(2)}) copy-start(f32[4,1792]{1,0:T(4,128)} %param.17) | copy-start | bytes 86020
  82.6 8.9 %copy-start.5 = (bf16[128,3328]{1,0:T(8,128)(2,1)}, bf16[128,3328]{1,0:T(8,128)(2,1)S(1)}, u32[]{:S(2)}) copy-start(bf16[128,3328]{1,0:T(8,128)(2,1)S(1)} %convolution_convert_fusion) | copy-start | bytes 2555908
  82.7 4.8 collective-permute-start
  86.1 2.9 copy-start.10
  86.1 2.9 copy-start.12
  86.1 2.9 copy-start.14
  86.2 2.9 copy-start.16
  89.1 123.4 %copy-start.3 = (bf16[128,1792]{1,0:T(8,128)(2,1)}, bf16[128,1792]{1,0:T(8,128)(2,1)S(1)}, u32[]{:S(2)}) copy-start(bf16[128,1792]{1,0:T(8,128)(2,1)S(1)} %get-tuple-element.403) | copy-start | bytes 1376260
  91.5 1.3 copy-start.17
  94.5 7.9 %copy-start.20 = (f32[24]{0:T(128)S(1)}, f32[24]{0:T(128)}, u32[]{:S(2)}) copy-start(f32[24]{0:T(128)} %param.18) | copy-start | bytes 292
  94.5 117.9 %all-to-all-start = ((bf16[32,48,768]{2,1,0:T(8,128)(2,1)}), bf16[32,48,768]{2,1,0:T(8,128)(2,1)}, u32[]{:S(2)}, u32[]{:S(2)}) async-start(bf16[32,48,768]{2,1,0:T(8,128)(2,1)} %stack.2), calls=%async_computation | async-start | bytes 4718592 | tf_op jit(solution)/shard_map/all_to_all | solution.py:12
  102.2 386.8 %all-reduce.12.cloned.1.call-start = ((), (), s32[]{:S(2)}) async-start(), calls=%async_computation.4 | async-start | bytes 9437184
  210.9 1.6 copy-start.18
  216.5 3.1 copy-start.1
  219.5 341.0 %all-gather.12.cloned.1.call-start = ((), (), s32[]{:S(2)}) async-start(), calls=%async_computation.3 | async-start | bytes 3538944 | tf_op jit(solution)/shard_map/all_gather | solution.py:40
  259.5 1.6 copy-start.9
  261.1 4.5 copy-start.2
  570.7 2.5 copy-start.4
  570.7 2.5 copy-start.6
  572.0 1.2 copy-start.7
  573.2 1.7 copy-start.11
  573.2 1.7 copy-start.13
  573.2 1.7 copy-start.15
  574.9 6.4 %slice-start = ((s8[5111808]{0:T(1024)(128)(4,1)}), s8[4194304]{0:T(1024)(128)(4,1)S(1)}, s32[]{:S(2)}) async-start(s8[5111808]{0:T(1024)(128)(4,1)} %bitcast.118), calls=%async_computation.5 | async-start | bytes 8388608
  575.1 6.2 %slice-start.1 = ((s8[5111808]{0:T(1024)(128)(4,1)}), s8[917504]{0:T(1024)(128)(4,1)S(1)}, s32[]{:S(2)}) async-start(s8[5111808]{0:T(1024)(128)(4,1)} %bitcast.118), calls=%async_computation.6 | async-start | bytes 1835008
  575.1 6.2 %copy-start.8 = (bf16[128,1536]{1,0:T(8,128)(2,1)S(1)}, bf16[128,1536]{1,0:T(8,128)(2,1)}, u32[]{:S(2)}) copy-start(bf16[128,1536]{1,0:T(8,128)(2,1)} %get-tuple-element.405) | copy-start | bytes 1179652
  575.2 6.0 %collective-permute-start.1 = (f32[3,1792]{1,0:T(4,128)S(1)}, f32[3,1792]{1,0:T(4,128)S(1)}, u32[]{:S(2)}, u32[]{:S(2)}) collective-permute-start(f32[3,1792]{1,0:T(4,128)S(1)} %pad_add_fusion.1), channel_id=1, source_target_pairs={{32,0},{64,32},{96,64},{128,96},{160,128},{192,160},{224,192},{33,... | collective-permute-start | bytes 64520 | tf_op jit(solution)/shard_map/ppermute | solution.py:18
Sparse Core Ops, SparseCore 0:
  9.8 69.3 all-gather.7
  93.0 108.4 all-gather.9
  219.6 269.3 all-reduce.11
  491.5 68.9 all-gather.11
